TPU v7x, 512 devices: a whole 4x4x16 slice. The times are simulated.
512 devices in a mesh: chan: 64 (over y, x, z_hi, core), freq: 8 (over z_lo).
Axes of the slice: x: 4, y: 4, z: 16 (z_hi: 2, z_lo: 8; z = z_hi * 8 + z_lo), core: 2. Of those that a mesh axis runs over, the one named last changes fastest.
Arguments:
- spectra: bfloat16 [256, 2, 16, 8192], P('freq', None, None, 'chan'), may hold values from -20 to 20
- model: bfloat16 [256, 2, 8, 8192], P('freq', None, None, 'chan'), may hold values from -6 to 6
- channel_ok: int32 [8192], replicated, may hold values 0 or 1
- limits: int32 [64], replicated, may hold values from 128 to 1024, as said below
Outputs:
- adjoint: float32 [256, 2, 16, 8192], P('freq', None, None, 'chan')
- misfit: float32 [], replicated
Inputs may be any that keep to these rules, and one draw needn't show every extreme that they name: `limits`: one block has the limit 128 and another the limit 1024.
All inputs are finite; a program needn't handle non-finite values.
Results may differ from a plain program's by a relative error of at most 0.00053.
Values may be sent and summed in bfloat16 or wider, within the bound.
A program may use at most 64 MiB of HBM per device.

v0:
```python
import jax
import jax.numpy as jnp
from jax import lax
from jax.sharding import PartitionSpec as P

F = 256
W = 16
BAND = 1024
GROUP = 4


def permute(x, pairs):
    return lax.ppermute(x, "chan", pairs)


def shift_pairs(peers, by):
    return [(i, (i + by) % peers) for i in range(peers)]


def group_pairs(peers, t):
    return [(i, i // GROUP * GROUP + (i % GROUP + t) % GROUP) for i in range(peers)]


def exchange(chunks, j, peers):
    rel = jnp.roll(chunks, -j, axis=0)
    got = [rel[0]] + [permute(rel[t], group_pairs(peers, t)) for t in range(1, GROUP)]
    got = jnp.stack(got, axis=0)
    order = (j - jnp.arange(GROUP)) % GROUP
    return jnp.take(got, order, axis=0)


def pair_terms(first, second, ok_first, ok_second, limit_first, shift_blocks):
    row_count = first.shape[2]
    block_width = first.shape[4]
    row_scale = jnp.concatenate(
        [jnp.full((W,), 1.0 / W, jnp.float32), jnp.full((row_count - W,), -1.0, jnp.float32)]
    ).astype(jnp.bfloat16)
    scaled = first * row_scale[None, None, :, None, None]
    fb = first.shape[0]
    nb = first.shape[3]
    stacked_left = jnp.stack(
        [
            scaled.reshape(fb, 2 * row_count, nb, block_width),
            jnp.concatenate([scaled[:, 1], -scaled[:, 0]], axis=1),
        ],
        axis=0,
    )
    right_rows = second.reshape(fb, 2 * row_count, nb, block_width)
    cross_spec = jnp.einsum(
        "xfrbc,frbd->xfbcd", stacked_left, right_rows, preferred_element_type=jnp.float32
    )
    row_index = lax.broadcasted_iota(jnp.int32, (block_width, block_width), 0)
    col_index = lax.broadcasted_iota(jnp.int32, (block_width, block_width), 1)
    offset = shift_blocks * block_width + col_index - row_index
    inside = ((offset[None] >= 1) & (offset[None] <= limit_first[:, None, None])).astype(
        jnp.float32
    )
    live_mask = ok_first[:, :, None] * ok_second[:, None, :] * inside
    residual = cross_spec * live_mask[None, None]
    piece_loss = 0.5 * jnp.sum(residual * residual)
    rounded = residual.astype(jnp.bfloat16)
    far_spec = second[:, :, :W].reshape(fb, 2 * W, nb, block_width)
    near_spec = first[:, :, :W].reshape(fb, 2 * W, nb, block_width)
    toward = jnp.einsum("xfbcd,fvbd->xfvbc", rounded, far_spec, preferred_element_type=jnp.float32)
    first_real = toward[0, :, :W] - toward[1, :, W:]
    first_imag = toward[0, :, W:] + toward[1, :, :W]
    backward = jnp.einsum(
        "xfbcd,fvbc->xfvbd", rounded, near_spec, preferred_element_type=jnp.float32
    )
    second_real = backward[0, :, :W] + backward[1, :, W:]
    second_imag = backward[0, :, W:] - backward[1, :, :W]
    return (
        piece_loss,
        jnp.stack([first_real, first_imag], axis=1),
        jnp.stack([second_real, second_imag], axis=1),
    )


def shards(spectra, model, channel_ok, limits):
    payload = jnp.concatenate([spectra, model], axis=2)
    fl, _, rows, bw = payload.shape
    peers = lax.axis_size("chan")
    me = lax.axis_index("chan")
    j = me % GROUP
    column = me // GROUP
    sub = fl // GROUP
    band_blocks = BAND // bw
    halo_cols = -(-band_blocks // GROUP)
    span = GROUP * bw
    chunks = payload.reshape(GROUP, sub, 2, rows, bw)
    mine = exchange(chunks, j, peers)
    own = jnp.transpose(mine, (1, 2, 3, 0, 4)).reshape(sub, 2, rows, span)
    parts = [own] + [permute(own, shift_pairs(peers, -GROUP * h)) for h in range(1, halo_cols + 1)]
    ext = jnp.concatenate(parts, axis=3)
    total = ext.shape[3]
    ok_all = channel_ok.astype(jnp.float32)
    ok_wide = jnp.concatenate([ok_all, ok_all[:total]])
    ok_ext = lax.dynamic_slice_in_dim(ok_wide, column * span, total)
    lim = lax.dynamic_slice_in_dim(limits, column * GROUP, GROUP)
    first = ext[:, :, :, :span].reshape(sub, 2, rows, GROUP, bw)
    ok_first = ok_ext[:span].reshape(GROUP, bw)
    misfit_sum = jnp.zeros((), jnp.float32)
    near_acc = jnp.zeros((sub, 2, W, GROUP, bw), jnp.float32)
    far_acc = jnp.zeros((sub, 2, W, total), jnp.float32)
    for s in range(band_blocks + 1):
        second = ext[:, :, :, s * bw : s * bw + span].reshape(sub, 2, rows, GROUP, bw)
        ok_second = ok_ext[s * bw : s * bw + span].reshape(GROUP, bw)
        piece_loss, near_terms, far_terms = pair_terms(first, second, ok_first, ok_second, lim, s)
        misfit_sum = misfit_sum + piece_loss
        near_acc = near_acc + near_terms
        far_flat = far_terms.reshape(sub, 2, W, span)
        far_acc = far_acc + jnp.pad(
            far_flat, ((0, 0), (0, 0), (0, 0), (s * bw, total - span - s * bw))
        )
    adj = near_acc.reshape(sub, 2, W, span) + far_acc[:, :, :, :span]
    for h in range(1, halo_cols + 1):
        adj = adj + permute(
            far_acc[:, :, :, h * span : (h + 1) * span], shift_pairs(peers, GROUP * h)
        )
    adj = adj * (1.0 / W)
    blocks = jnp.transpose(adj.reshape(sub, 2, W, GROUP, bw), (3, 0, 1, 2, 4))
    back = exchange(blocks, j, peers)
    adjoint = back.reshape(fl, 2, W, bw)
    misfit_total = lax.psum(misfit_sum, ("chan", "freq"))
    misfit = misfit_total / float(F * bw * peers * BAND)
    return (adjoint, misfit)


def solution(mesh):
    return jax.shard_map(
        shards,
        mesh=mesh,
        in_specs=(P("freq", None, None, "chan"), P("freq", None, None, "chan"), P(), P()),
        out_specs=(P("freq", None, None, "chan"), P()),
        check_vma=False,
    )
```

profile of v0, /device:TPU:1, one launch (start us, length us, event | category | flops | bytes accessed | tf_op | source)
XLA Modules:
  0.0 330.2 jit_solution(5131253265094476053)
XLA Ops:
  0.7 1.1 pad_maximum_fusion.2
  2.6 16.3 %collective-permute-start.1 = (bf16[8,2,24,128]{3,2,1,0:T(8,128)(2,1)}, bf16[8,2,24,128]{3,2,1,0:T(8,128)(2,1)S(1)}, u32[]{:S(2)}, u32[]{:S(2)}) collective-permute-start(bf16[8,2,24,128]{3,2,1,0:T(8,128)(2,1)} %get-tuple-element.57), channel_id=1, source_target_pairs={{0,16},{8,24},{16,0},{24,8},{32,48},{40,56},{48,32},{56,40},{64,80... | collective-permute-start | bytes 294920 | tf_op jit(solution)/shard_map/ppermute | solution.py:13
  18.9 4.8 %collective-permute-start = (bf16[8,2,24,128]{3,2,1,0:T(8,128)(2,1)S(1)}, bf16[8,2,24,128]{3,2,1,0:T(8,128)(2,1)S(1)}, u32[]{:S(2)}, u32[]{:S(2)}) collective-permute-start(bf16[8,2,24,128]{3,2,1,0:T(8,128)(2,1)S(1)} %get-tuple-element.58), channel_id=1, source_target_pairs={{0,8},{8,16},{16,24},{24,0},{32,40},{40,48},{48,56},{56,32},{64,72... | collective-permute-start | bytes 294920 | tf_op jit(solution)/shard_map/ppermute | solution.py:13
  23.6 1.9 collective-permute-start.2
  28.4 1.2 multiply_select_fusion.8
  29.6 9.8 %collective-permute-done.2 = bf16[8,2,24,128]{3,2,1,0:T(8,128)(2,1)} collective-permute-done((bf16[8,2,24,128]{3,2,1,0:T(8,128)(2,1)S(1)}, bf16[8,2,24,128]{3,2,1,0:T(8,128)(2,1)}, u32[]{:S(2)}, u32[]{:S(2)}) %collective-permute-start.2) | collective-permute-done | bytes 98336 | tf_op jit(solution)/shard_map/ppermute | solution.py:13
  39.4 0.9 pad_maximum_fusion.3
  40.3 1.5 gather_fusion
  41.8 1.1 broadcast_multiply_fusion
  43.8 0.9 copy.35
  45.5 1.9 reshape.1311
  47.4 7.6 %collective-permute-start.4 = (bf16[8,2,24,512]{3,2,1,0:T(8,128)(2,1)}, bf16[8,2,24,512]{3,2,1,0:T(8,128)(2,1)S(1)}, u32[]{:S(2)}, u32[]{:S(2)}) collective-permute-start(bf16[8,2,24,512]{3,2,1,0:T(8,128)(2,1)} %reshape.1311), channel_id=1, source_target_pairs={{0,448},{8,456},{16,464},{24,472},{32,480},{40,488},{48,496},{56,5... | collective-permute-start | bytes 1179656 | tf_op jit(solution)/shard_map/ppermute | solution.py:13
  55.0 3.2 collective-permute-start.3
  58.3 1.1 maximum_bitcast_fusion
  59.4 2.9 multiply_reduce_fusion.8
  62.3 0.9 convolution_bitcast_fusion.8
  67.0 1.0 constant_dynamic-update-slice_fusion.1
  68.1 4.6 %collective-permute-done.3 = bf16[8,2,24,512]{3,2,1,0:T(8,128)(2,1)S(1)} collective-permute-done((bf16[8,2,24,512]{3,2,1,0:T(8,128)(2,1)}, bf16[8,2,24,512]{3,2,1,0:T(8,128)(2,1)S(1)}, u32[]{:S(2)}, u32[]{:S(2)}) %collective-permute-start.3) | collective-permute-done | bytes 393248 | tf_op jit(solution)/shard_map/ppermute | solution.py:13
  73.6 1.1 fusion.71
  74.7 0.9 copy-done.5
  75.6 1.8 reshape_reshape.24
  77.4 1.8 reshape.1312
  79.2 1.8 reshape_reshape.26
  81.1 1.8 reshape.1316
  83.8 0.9 reshape.1314
  84.6 2.3 fusion.72
  87.7 0.9 reshape_reshape.28
  88.5 1.9 reshape.1320
  90.4 1.9 reshape_reshape.30
  92.3 1.9 reshape.1324
  94.1 1.8 reshape_reshape.29
  96.0 1.8 reshape.1322
  98.6 1.0 slice.638
  100.4 1.8 reshape.1318
  102.3 1.1 slice.611
  104.2 1.0 slice.591
  108.5 1.9 multiply_reduce_fusion.6
  110.3 0.9 convolution_bitcast_fusion.6
  115.1 2.0 multiply_reduce_fusion.5
  117.1 0.9 convolution_bitcast_fusion.5
  122.7 3.0 multiply_reduce_fusion.4
  125.7 1.0 convolution_bitcast_fusion.4
  129.2 1.9 multiply_reduce_fusion.3
  131.1 0.9 convolution_bitcast_fusion.3
  135.2 1.9 multiply_reduce_fusion.2
  137.1 0.9 convolution_bitcast_fusion.2
  141.2 0.8 copy.65
  142.0 1.9 multiply_reduce_fusion.1
  143.9 0.9 convolution_bitcast_fusion.1
  148.8 1.9 multiply_reduce_fusion.7
  154.5 1.9 multiply_reduce_fusion
  156.4 0.8 convolution_bitcast_fusion
  158.9 4.2 %fusion.9 = f32[8,2,16,1536]{3,1,2,0:T(2,128)S(1)} fusion(f32[8,1,16,512]{3,1,2,0:T(1,128)S(1)} %bitcast.366, f32[8,1,16,512]{3,1,2,0:T(1,128)S(1)} %bitcast.364, f32[8,1,16,512]{3,1,2,0:T(1,128)S(1)} %bitcast.360, f32[8,1,16,512]{3,1,2,0:T(1,128)S(1)} %bitcast.359, f32[8,1,16,512]{3,1,2,0:T(1,128)S(1)} %bitcast.357, f32[8,1,16,512]{3,1,2,0:T(1,128)S(1)} %bitcast.356, ...), kind=kLoop, calls=%fused_computation.37 | loop fusion | flops 22806528 | bytes 6291456 | tf_op jit(solution)/shard_map/add | solution.py:112
  163.7 1.9 collective-permute-start.5
  165.6 4.7 %collective-permute-start.6 = (f32[8,2,16,512]{3,1,2,0:T(2,128)S(1)}, f32[8,2,16,512]{3,1,2,0:T(2,128)S(1)}, u32[]{:S(2)}, u32[]{:S(2)}) collective-permute-start(f32[8,2,16,512]{3,1,2,0:T(2,128)S(1)} %get-tuple-element.5), channel_id=1, source_target_pairs={{0,64},{8,72},{16,80},{24,88},{32,96},{40,104},{48,112},{56,120},{... | collective-permute-start | bytes 1572872 | tf_op jit(solution)/shard_map/ppermute | solution.py:13
  171.3 10.8 %collective-permute-done.5 = f32[8,2,16,512]{3,1,2,0:T(2,128)S(1)} collective-permute-done((f32[8,2,16,512]{3,1,2,0:T(2,128)S(1)}, f32[8,2,16,512]{3,1,2,0:T(2,128)S(1)}, u32[]{:S(2)}, u32[]{:S(2)}) %collective-permute-start.5) | collective-permute-done | bytes 524320 | tf_op jit(solution)/shard_map/ppermute | solution.py:13
  182.1 12.8 %collective-permute-done.6 = f32[8,2,16,512]{3,1,2,0:T(2,128)S(1)} collective-permute-done((f32[8,2,16,512]{3,1,2,0:T(2,128)S(1)}, f32[8,2,16,512]{3,1,2,0:T(2,128)S(1)}, u32[]{:S(2)}, u32[]{:S(2)}) %collective-permute-start.6) | collective-permute-done | bytes 524320 | tf_op jit(solution)/shard_map/ppermute | solution.py:13
  195.0 4.5 %fusion.38 = f32[8,2,16,512]{3,1,2,0:T(2,128)S(1)} fusion(f32[8,2,16,512]{3,1,2,0:T(2,128)S(1)} %collective-permute-done.6, f32[8,2,16,512]{3,1,2,0:T(2,128)S(1)} %collective-permute-done.5, f32[8,2,16,1536]{3,1,2,0:T(2,128)S(1)} %fusion.9, f32[8,1,16,512]{3,1,2,0:T(1,128)S(1)} %bitcast.380, f32[8,1,16,512]{3,1,2,0:T(1,128)S(1)} %bitcast.379, ...), kind=kLoop, calls=%fused_computation.80 | loop fusion | flops 2752512 | bytes 6815744 | tf_op jit(solution)/shard_map/mul | solution.py:120
  200.8 3.2 collective-permute-start.9
  204.1 1.9 collective-permute-start.8
  206.0 12.3 %collective-permute-start.7 = (f32[8,2,16,128]{3,1,2,0:T(2,128)S(1)}, f32[8,2,16,128]{3,1,2,0:T(2,128)S(1)}, u32[]{:S(2)}, u32[]{:S(2)}) collective-permute-start(f32[8,2,16,128]{3,1,2,0:T(2,128)S(1)} %bitcast.386), channel_id=1, source_target_pairs={{0,8},{8,16},{16,24},{24,0},{32,40},{40,48},{48,56},{56,32},{64,72... | collective-permute-start | bytes 393224 | tf_op jit(solution)/shard_map/ppermute | solution.py:13
  224.0 101.7 %psum.7 = f32[]{:T(128)} all-reduce(f32[]{:T(128)S(6)} %add.589), channel_id=1, replica_groups=mesh['chan'=64,'freq'=8] {'chan','freq'}, use_global_device_ids=true, to_apply=%region_9.10 | all-reduce | flops 1 | bytes 8 | tf_op jit(solution)/shard_map/psum | solution.py:124
  326.7 1.2 gather_fusion.1
  328.0 0.9 bitcast_select_fusion
  (227 shorter events, 47.0 us)
Async XLA Ops:
  0.6 26.7 %copy-start.45 = (s32[8192]{0:T(1024)S(1)}, s32[8192]{0:T(1024)}, u32[]{:S(2)}) copy-start(s32[8192]{0:T(1024)} %param.6) | copy-start | bytes 98308
  0.6 27.3 %copy-start.46 = (s32[64]{0:T(128)S(1)}, s32[64]{0:T(128)}, u32[]{:S(2)}) copy-start(s32[64]{0:T(128)} %param.7) | copy-start | bytes 772
  2.6 26.9 %collective-permute-start.1 = (bf16[8,2,24,128]{3,2,1,0:T(8,128)(2,1)}, bf16[8,2,24,128]{3,2,1,0:T(8,128)(2,1)S(1)}, u32[]{:S(2)}, u32[]{:S(2)}) collective-permute-start(bf16[8,2,24,128]{3,2,1,0:T(8,128)(2,1)} %get-tuple-element.57), channel_id=1, source_target_pairs={{0,16},{8,24},{16,0},{24,8},{32,48},{40,56},{48,32},{56,40},{64,80... | collective-permute-start | bytes 294920 | tf_op jit(solution)/shard_map/ppermute | solution.py:13
  18.9 10.7 %collective-permute-start = (bf16[8,2,24,128]{3,2,1,0:T(8,128)(2,1)S(1)}, bf16[8,2,24,128]{3,2,1,0:T(8,128)(2,1)S(1)}, u32[]{:S(2)}, u32[]{:S(2)}) collective-permute-start(bf16[8,2,24,128]{3,2,1,0:T(8,128)(2,1)S(1)} %get-tuple-element.58), channel_id=1, source_target_pairs={{0,8},{8,16},{16,24},{24,0},{32,40},{40,48},{48,56},{56,32},{64,72... | collective-permute-start | bytes 294920 | tf_op jit(solution)/shard_map/ppermute | solution.py:13
  23.6 15.7 %collective-permute-start.2 = (bf16[8,2,24,128]{3,2,1,0:T(8,128)(2,1)S(1)}, bf16[8,2,24,128]{3,2,1,0:T(8,128)(2,1)}, u32[]{:S(2)}, u32[]{:S(2)}) collective-permute-start(bf16[8,2,24,128]{3,2,1,0:T(8,128)(2,1)S(1)} %get-tuple-element.59), channel_id=1, source_target_pairs={{0,24},{8,0},{16,8},{24,16},{32,56},{40,32},{48,40},{56,48},{64,88... | collective-permute-start | bytes 294920 | tf_op jit(solution)/shard_map/ppermute | solution.py:13
  47.4 25.4 %collective-permute-start.4 = (bf16[8,2,24,512]{3,2,1,0:T(8,128)(2,1)}, bf16[8,2,24,512]{3,2,1,0:T(8,128)(2,1)S(1)}, u32[]{:S(2)}, u32[]{:S(2)}) collective-permute-start(bf16[8,2,24,512]{3,2,1,0:T(8,128)(2,1)} %reshape.1311), channel_id=1, source_target_pairs={{0,448},{8,456},{16,464},{24,472},{32,480},{40,488},{48,496},{56,5... | collective-permute-start | bytes 1179656 | tf_op jit(solution)/shard_map/ppermute | solution.py:13
  55.0 17.7 %collective-permute-start.3 = (bf16[8,2,24,512]{3,2,1,0:T(8,128)(2,1)}, bf16[8,2,24,512]{3,2,1,0:T(8,128)(2,1)S(1)}, u32[]{:S(2)}, u32[]{:S(2)}) collective-permute-start(bf16[8,2,24,512]{3,2,1,0:T(8,128)(2,1)} %reshape.1311), channel_id=1, source_target_pairs={{0,480},{8,488},{16,496},{24,504},{32,0},{40,8},{48,16},{56,24},{6... | collective-permute-start | bytes 1179656 | tf_op jit(solution)/shard_map/ppermute | solution.py:13
  72.7 1.9 copy-start.3
  72.8 0.8 copy-start
  74.7 0.9 copy-start.5
  86.9 0.8 copy-start.2
  88.5 9.3 %copy-start.1 = (bf16[8,2,24,512]{3,2,1,0:T(8,128)(2,1)S(1)}, bf16[8,2,24,512]{3,2,1,0:T(8,128)(2,1)}, u32[]{:S(2)}) copy-start(bf16[8,2,24,512]{3,2,1,0:T(8,128)(2,1)} %copy-done) | copy-start | bytes 1179652
  102.3 3.7 %slice-start.1 = ((bf16[8,2,24,4,128]{4,3,2,1,0:T(4,128)(2,1)}), bf16[8,2,16,4,128]{4,3,2,1,0:T(4,128)(2,1)S(1)}, s32[]{:S(2)}) async-start(bf16[8,2,24,4,128]{4,3,2,1,0:T(4,128)(2,1)} %reshape.1316), calls=%async_computation.1 | async-start | bytes 524288 | tf_op jit(solution)/shard_map/slice | solution.py:62
  102.3 3.8 %slice-start = ((bf16[8,2,24,4,128]{4,3,2,1,0:T(4,128)(2,1)}), bf16[8,2,16,4,128]{4,3,2,1,0:T(4,128)(2,1)S(1)}, s32[]{:S(2)}) async-start(bf16[8,2,24,4,128]{4,3,2,1,0:T(4,128)(2,1)} %reshape.1314), calls=%async_computation | async-start | bytes 524288 | tf_op jit(solution)/shard_map/slice | solution.py:62
  103.4 2.7 slice-start.4
  105.2 1.7 slice-start.2
  106.0 1.6 slice-start.3
  106.1 2.4 copy-start.11
  111.8 3.3 %copy-start.10 = (bf16[8,48,4,128]{3,2,1,0:T(4,128)(2,1)S(1)}, bf16[8,48,4,128]{3,2,1,0:T(4,128)(2,1)}, u32[]{:S(2)}) copy-start(bf16[8,48,4,128]{3,2,1,0:T(4,128)(2,1)} %reshape_reshape.26) | copy-start | bytes 1179652
  118.5 3.3 %copy-start.4 = (bf16[8,2,24,512]{3,2,1,0:T(8,128)(2,1)S(1)}, bf16[8,2,24,512]{3,2,1,0:T(8,128)(2,1)}, u32[]{:S(2)}) copy-start(bf16[8,2,24,512]{3,2,1,0:T(8,128)(2,1)} %copy-done.3) | copy-start | bytes 1179652
  125.6 1.0 copy-start.26
  127.2 1.9 copy-start.9
  131.1 0.9 copy-start.23
  132.6 2.6 copy-start.8
  137.1 0.9 copy-start.21
  138.7 3.4 %copy-start.7 = (bf16[8,48,4,128]{3,2,1,0:T(4,128)(2,1)S(1)}, bf16[8,48,4,128]{3,2,1,0:T(4,128)(2,1)}, u32[]{:S(2)}) copy-start(bf16[8,48,4,128]{3,2,1,0:T(4,128)(2,1)} %reshape_reshape.30) | copy-start | bytes 1179652
  143.9 0.9 copy-start.20
  145.5 3.3 %copy-start.6 = (bf16[8,48,4,128]{3,2,1,0:T(4,128)(2,1)S(1)}, bf16[8,48,4,128]{3,2,1,0:T(4,128)(2,1)}, u32[]{:S(2)}) copy-start(bf16[8,48,4,128]{3,2,1,0:T(4,128)(2,1)} %reshape_reshape.24) | copy-start | bytes 1179652
  150.7 0.9 copy-start.16
  156.4 1.3 copy-start.28
  157.3 1.0 copy-start.12
  157.3 1.1 copy-start.13
  157.3 1.1 copy-start.15
  157.3 1.2 copy-start.17
  157.3 1.3 copy-start.18
  157.3 1.3 copy-start.19
  157.3 1.4 copy-start.22
  157.3 1.5 copy-start.24
  157.3 1.5 copy-start.25
  157.4 1.6 copy-start.27
  163.1 7.2 %copy-start.14 = (bf16[8,2,16,4,128]{4,2,1,3,0:T(8,128)(2,1)S(1)}, bf16[8,2,16,4,128]{4,2,1,3,0:T(8,128)(2,1)}, u32[]{:S(2)}) copy-start(bf16[8,2,16,4,128]{4,2,1,3,0:T(8,128)(2,1)} %copy.71) | copy-start | bytes 786436
  163.7 18.4 %collective-permute-start.5 = (f32[8,2,16,512]{3,1,2,0:T(2,128)S(1)}, f32[8,2,16,512]{3,1,2,0:T(2,128)S(1)}, u32[]{:S(2)}, u32[]{:S(2)}) collective-permute-start(f32[8,2,16,512]{3,1,2,0:T(2,128)S(1)} %get-tuple-element.4), channel_id=1, source_target_pairs={{0,32},{8,40},{16,48},{24,56},{32,64},{40,72},{48,80},{56,88},{64,... | collective-permute-start | bytes 1572872 | tf_op jit(solution)/shard_map/ppermute | solution.py:13
  165.6 29.2 %collective-permute-start.6 = (f32[8,2,16,512]{3,1,2,0:T(2,128)S(1)}, f32[8,2,16,512]{3,1,2,0:T(2,128)S(1)}, u32[]{:S(2)}, u32[]{:S(2)}) collective-permute-start(f32[8,2,16,512]{3,1,2,0:T(2,128)S(1)} %get-tuple-element.5), channel_id=1, source_target_pairs={{0,64},{8,72},{16,80},{24,88},{32,96},{40,104},{48,112},{56,120},{... | collective-permute-start | bytes 1572872 | tf_op jit(solution)/shard_map/ppermute | solution.py:13
  170.3 24.5 %copy-start.39 = (f32[1,8,16,4,128]{4,3,0,2,1:T(4,128)S(1)}, f32[1,8,16,4,128]{4,3,0,2,1:T(4,128)}, u32[]{:S(2)}) copy-start(f32[1,8,16,4,128]{4,3,0,2,1:T(4,128)} %copy.64) | copy-start | bytes 786436
  170.4 24.5 %copy-start.40 = (f32[1,8,16,4,128]{4,3,0,2,1:T(4,128)S(1)}, f32[1,8,16,4,128]{4,3,0,2,1:T(4,128)}, u32[]{:S(2)}) copy-start(f32[1,8,16,4,128]{4,3,0,2,1:T(4,128)} %copy.65) | copy-start | bytes 786436
  170.4 24.5 %copy-start.41 = (f32[1,8,16,4,128]{4,3,0,2,1:T(4,128)S(1)}, f32[1,8,16,4,128]{4,3,0,2,1:T(4,128)}, u32[]{:S(2)}) copy-start(f32[1,8,16,4,128]{4,3,0,2,1:T(4,128)} %copy.69) | copy-start | bytes 786436
  170.4 24.5 %copy-start.42 = (f32[1,8,16,4,128]{4,3,0,2,1:T(4,128)S(1)}, f32[1,8,16,4,128]{4,3,0,2,1:T(4,128)}, u32[]{:S(2)}) copy-start(f32[1,8,16,4,128]{4,3,0,2,1:T(4,128)} %copy.70) | copy-start | bytes 786436
  170.4 24.5 %copy-start.43 = (f32[1,8,16,4,128]{4,3,0,2,1:T(4,128)S(1)}, f32[1,8,16,4,128]{4,3,0,2,1:T(4,128)}, u32[]{:S(2)}) copy-start(f32[1,8,16,4,128]{4,3,0,2,1:T(4,128)} %copy.39) | copy-start | bytes 786436
  170.4 24.5 %copy-start.44 = (f32[1,8,16,4,128]{4,3,0,2,1:T(4,128)S(1)}, f32[1,8,16,4,128]{4,3,0,2,1:T(4,128)}, u32[]{:S(2)}) copy-start(f32[1,8,16,4,128]{4,3,0,2,1:T(4,128)} %copy.40) | copy-start | bytes 786436
  170.9 24.0 %copy-start.29 = (f32[1,8,16,4,128]{4,3,0,2,1:T(4,128)S(1)}, f32[1,8,16,4,128]{4,3,0,2,1:T(4,128)}, u32[]{:S(2)}) copy-start(f32[1,8,16,4,128]{4,3,0,2,1:T(4,128)} %copy.33) | copy-start | bytes 786436
  170.9 24.0 %copy-start.30 = (f32[1,8,16,4,128]{4,3,0,2,1:T(4,128)S(1)}, f32[1,8,16,4,128]{4,3,0,2,1:T(4,128)}, u32[]{:S(2)}) copy-start(f32[1,8,16,4,128]{4,3,0,2,1:T(4,128)} %copy.34) | copy-start | bytes 786436
  170.9 24.0 %copy-start.31 = (f32[1,8,16,4,128]{4,3,0,2,1:T(4,128)S(1)}, f32[1,8,16,4,128]{4,3,0,2,1:T(4,128)}, u32[]{:S(2)}) copy-start(f32[1,8,16,4,128]{4,3,0,2,1:T(4,128)} %copy.44) | copy-start | bytes 786436
  170.9 24.0 %copy-start.32 = (f32[1,8,16,4,128]{4,3,0,2,1:T(4,128)S(1)}, f32[1,8,16,4,128]{4,3,0,2,1:T(4,128)}, u32[]{:S(2)}) copy-start(f32[1,8,16,4,128]{4,3,0,2,1:T(4,128)} %copy.45) | copy-start | bytes 786436
  170.9 24.0 %copy-start.33 = (f32[1,8,16,4,128]{4,3,0,2,1:T(4,128)S(1)}, f32[1,8,16,4,128]{4,3,0,2,1:T(4,128)}, u32[]{:S(2)}) copy-start(f32[1,8,16,4,128]{4,3,0,2,1:T(4,128)} %copy.49) | copy-start | bytes 786436
  170.9 24.0 %copy-start.34 = (f32[1,8,16,4,128]{4,3,0,2,1:T(4,128)S(1)}, f32[1,8,16,4,128]{4,3,0,2,1:T(4,128)}, u32[]{:S(2)}) copy-start(f32[1,8,16,4,128]{4,3,0,2,1:T(4,128)} %copy.50) | copy-start | bytes 786436
  171.0 24.0 %copy-start.35 = (f32[1,8,16,4,128]{4,3,0,2,1:T(4,128)S(1)}, f32[1,8,16,4,128]{4,3,0,2,1:T(4,128)}, u32[]{:S(2)}) copy-start(f32[1,8,16,4,128]{4,3,0,2,1:T(4,128)} %copy.54) | copy-start | bytes 786436
  171.0 24.0 %copy-start.36 = (f32[1,8,16,4,128]{4,3,0,2,1:T(4,128)S(1)}, f32[1,8,16,4,128]{4,3,0,2,1:T(4,128)}, u32[]{:S(2)}) copy-start(f32[1,8,16,4,128]{4,3,0,2,1:T(4,128)} %copy.55) | copy-start | bytes 786436
  171.0 24.0 %copy-start.37 = (f32[1,8,16,4,128]{4,3,0,2,1:T(4,128)S(1)}, f32[1,8,16,4,128]{4,3,0,2,1:T(4,128)}, u32[]{:S(2)}) copy-start(f32[1,8,16,4,128]{4,3,0,2,1:T(4,128)} %copy.59) | copy-start | bytes 786436
  171.0 24.0 %copy-start.38 = (f32[1,8,16,4,128]{4,3,0,2,1:T(4,128)S(1)}, f32[1,8,16,4,128]{4,3,0,2,1:T(4,128)}, u32[]{:S(2)}) copy-start(f32[1,8,16,4,128]{4,3,0,2,1:T(4,128)} %copy.60) | copy-start | bytes 786436
  200.8 125.6 %collective-permute-start.9 = (f32[8,2,16,128]{3,1,2,0:T(2,128)S(1)}, f32[8,2,16,128]{3,1,2,0:T(2,128)S(1)}, u32[]{:S(2)}, u32[]{:S(2)}) collective-permute-start(f32[8,2,16,128]{3,1,2,0:T(2,128)S(1)} %bitcast.390), channel_id=1, source_target_pairs={{0,24},{8,0},{16,8},{24,16},{32,56},{40,32},{48,40},{56,48},{64,88... | collective-permute-start | bytes 393224 | tf_op jit(solution)/shard_map/ppermute | solution.py:13
  204.1 122.3 %collective-permute-start.8 = (f32[8,2,16,128]{3,1,2,0:T(2,128)S(1)}, f32[8,2,16,128]{3,1,2,0:T(2,128)S(1)}, u32[]{:S(2)}, u32[]{:S(2)}) collective-permute-start(f32[8,2,16,128]{3,1,2,0:T(2,128)S(1)} %bitcast.388), channel_id=1, source_target_pairs={{0,16},{8,24},{16,0},{24,8},{32,48},{40,56},{48,32},{56,40},{64,80... | collective-permute-start | bytes 393224 | tf_op jit(solution)/shard_map/ppermute | solution.py:13
  206.0 120.4 %collective-permute-start.7 = (f32[8,2,16,128]{3,1,2,0:T(2,128)S(1)}, f32[8,2,16,128]{3,1,2,0:T(2,128)S(1)}, u32[]{:S(2)}, u32[]{:S(2)}) collective-permute-start(f32[8,2,16,128]{3,1,2,0:T(2,128)S(1)} %bitcast.386), channel_id=1, source_target_pairs={{0,8},{8,16},{16,24},{24,0},{32,40},{40,48},{48,56},{56,32},{64,72... | collective-permute-start | bytes 393224 | tf_op jit(solution)/shard_map/ppermute | solution.py:13
where the time goes:
time: 334 us; the launch traced here: 330 us
  blocking collectives  102 us (31%)
  local copies, waits for them, and re-layouts  71.9 us (22%)
  starting transfers between devices  57.9 us (17%)
  waiting for transfers between devices  38 us (11%)
  matrix products  31.7 us (9%)
  other arithmetic  19.6 us (6%)
  between operations  9.45 us (3%)
    psum x1, blocking collectives, shards(): misfit_total = lax.psum(misfit_sum, ('chan', 'freq'))  102 us
    ppermute x10, starting transfers between devices, permute(): return lax.ppermute(x, 'chan', pairs)  57.9 us
    ppermute x10, waiting for transfers between devices, permute(): return lax.ppermute(x, 'chan', pairs)  38 us
    dot_general x9, matrix products, pair_terms(): jnp.einsum('xfrbc,frbd->xfbcd', stacked_left, right_rows, preferred_eleme...  19.3 us
    reshape x8, local copies, waits for them, and re-layouts, shards(): second = ext[:, :, :, s * bw:s * bw + span].reshape(sub, 2, rows, GROUP, bw)  12.8 us
    another operation x8, local copies, waits for them, and re-layouts, pair_terms(): right_rows = second.reshape(fb, 2 * row_count, nb, block_width)  9.99 us
    slice x23, local copies, waits for them, and re-layouts, pair_terms(): far_spec = second[:, :, :W].reshape(fb, 2 * W, nb, block_width)  7.92 us
    dot_general x9, matrix products, pair_terms(): jnp.einsum('xfbcd,fvbc->xfvbd', rounded, near_spec, preferred_element_typ...  7.82 us
  transfers between devices with their start and end apart: 10, of which 4 were waited for; matrix products, arithmetic and copies ran while one was open for 4% of the time, Pallas kernels for 0%

commit v1 on v0

--- a/solution.py
+++ b/solution.py
@@ -121,7 +121,7 @@
     blocks = jnp.transpose(adj.reshape(sub, 2, W, GROUP, bw), (3, 0, 1, 2, 4))
     back = exchange(blocks, j, peers)
     adjoint = back.reshape(fl, 2, W, bw)
-    misfit_total = lax.psum(misfit_sum, ("chan", "freq"))
+    misfit_total = lax.psum(lax.psum(misfit_sum, "freq"), "chan")
     misfit = misfit_total / float(F * bw * peers * BAND)
     return (adjoint, misfit)
 

time: 334 us -> 539 us (1.61)
  blocking collectives: 102 us -> 306 us
    psum x1 -> x2, blocking collectives: 102 us -> 306 us  [shards(): misfit_total = lax.psum(lax.psum(misfit_sum, 'freq'), 'chan')]
  transfers between devices with their start and end apart: 10 -> 10, of which waited for: 4 -> 4; matrix products, arithmetic and copies ran while one was open for 4% -> 3% of each run, Pallas kernels for 0% -> 0%
where the time goes in v1:
time: 539 us; the launch traced here: 535 us
  blocking collectives  306 us (57%)
  local copies, waits for them, and re-layouts  72 us (13%)
  starting transfers between devices  57.9 us (11%)
  waiting for transfers between devices  37.9 us (7%)
  matrix products  31.9 us (6%)
  other arithmetic  19.7 us (4%)
  between operations  9.61 us (2%)
    psum x2, blocking collectives, shards(): misfit_total = lax.psum(lax.psum(misfit_sum, 'freq'), 'chan')  306 us
    ppermute x10, starting transfers between devices, permute(): return lax.ppermute(x, 'chan', pairs)  57.9 us
    ppermute x10, waiting for transfers between devices, permute(): return lax.ppermute(x, 'chan', pairs)  37.9 us
    dot_general x9, matrix products, pair_terms(): jnp.einsum('xfrbc,frbd->xfbcd', stacked_left, right_rows, preferred_eleme...  19.4 us
    reshape x8, local copies, waits for them, and re-layouts, shards(): second = ext[:, :, :, s * bw:s * bw + span].reshape(sub, 2, rows, GROUP, bw)  12.8 us
  transfers between devices with their start and end apart: 10, of which 4 were waited for; matrix products, arithmetic and copies ran while one was open for 3% of the time, Pallas kernels for 0%

profile of v1, /device:TPU:1, one launch (start us, length us, event | category | flops | bytes accessed | tf_op | source)
XLA Modules:
  0.0 535.2 jit_solution(5669061030479656141)
XLA Ops:
  0.7 1.1 pad_maximum_fusion.2
  2.6 16.3 %collective-permute-start.1 = (bf16[8,2,24,128]{3,2,1,0:T(8,128)(2,1)}, bf16[8,2,24,128]{3,2,1,0:T(8,128)(2,1)S(1)}, u32[]{:S(2)}, u32[]{:S(2)}) collective-permute-start(bf16[8,2,24,128]{3,2,1,0:T(8,128)(2,1)} %get-tuple-element.57), channel_id=1, source_target_pairs={{0,16},{8,24},{16,0},{24,8},{32,48},{40,56},{48,32},{56,40},{64,80... | collective-permute-start | bytes 294920 | tf_op jit(solution)/shard_map/ppermute | solution.py:13
  18.9 4.8 collective-permute-start
  23.6 1.9 collective-permute-start.2
  28.4 1.2 multiply_select_fusion.8
  29.6 9.8 %collective-permute-done.2 = bf16[8,2,24,128]{3,2,1,0:T(8,128)(2,1)} collective-permute-done((bf16[8,2,24,128]{3,2,1,0:T(8,128)(2,1)S(1)}, bf16[8,2,24,128]{3,2,1,0:T(8,128)(2,1)}, u32[]{:S(2)}, u32[]{:S(2)}) %collective-permute-start.2) | collective-permute-done | bytes 98336 | tf_op jit(solution)/shard_map/ppermute | solution.py:13
  39.4 0.9 pad_maximum_fusion.3
  40.3 1.5 gather_fusion
  41.8 1.1 broadcast_multiply_fusion
  43.8 0.9 copy.35
  45.5 1.9 reshape.1311
  47.4 7.6 %collective-permute-start.4 = (bf16[8,2,24,512]{3,2,1,0:T(8,128)(2,1)}, bf16[8,2,24,512]{3,2,1,0:T(8,128)(2,1)S(1)}, u32[]{:S(2)}, u32[]{:S(2)}) collective-permute-start(bf16[8,2,24,512]{3,2,1,0:T(8,128)(2,1)} %reshape.1311), channel_id=1, source_target_pairs={{0,448},{8,456},{16,464},{24,472},{32,480},{40,488},{48,496},{56,5... | collective-permute-start | bytes 1179656 | tf_op jit(solution)/shard_map/ppermute | solution.py:13
  55.0 3.2 collective-permute-start.3
  58.3 1.1 maximum_bitcast_fusion
  59.4 3.0 multiply_reduce_fusion.8
  62.3 0.8 convolution_bitcast_fusion.8
  67.1 1.0 constant_dynamic-update-slice_fusion.1
  68.1 4.6 collective-permute-done.3
  73.6 1.1 fusion.71
  74.7 0.9 copy-done.5
  75.6 1.8 reshape_reshape.24
  77.5 1.8 reshape.1312
  79.3 1.8 reshape_reshape.26
  81.1 1.9 reshape.1316
  83.8 0.9 reshape.1314
  84.7 2.3 fusion.72
  88.6 1.9 reshape.1320
  90.5 1.9 reshape_reshape.30
  92.4 1.9 reshape.1324
  94.2 1.8 reshape_reshape.29
  96.1 1.8 reshape.1322
  98.8 1.0 slice.638
  100.6 1.8 reshape.1318
  102.4 1.1 slice.611
  104.3 1.0 slice.591
  108.6 1.9 multiply_reduce_fusion.6
  110.5 0.9 convolution_bitcast_fusion.6
  115.3 2.0 multiply_reduce_fusion.5
  117.2 0.9 convolution_bitcast_fusion.5
  122.8 2.9 multiply_reduce_fusion.4
  125.8 1.0 convolution_bitcast_fusion.4
  129.3 1.9 multiply_reduce_fusion.3
  131.2 0.9 convolution_bitcast_fusion.3
  135.3 2.0 multiply_reduce_fusion.2
  137.3 0.8 convolution_bitcast_fusion.2
  142.2 2.0 multiply_reduce_fusion.1
  144.2 0.9 convolution_bitcast_fusion.1
  149.1 1.9 multiply_reduce_fusion.7
  151.0 0.9 convolution_bitcast_fusion.7
  154.8 1.9 multiply_reduce_fusion
  156.7 0.8 convolution_bitcast_fusion
  159.2 4.2 fusion.9
  164.0 1.9 collective-permute-start.5
  165.9 4.7 collective-permute-start.6
  171.6 10.8 %collective-permute-done.5 = f32[8,2,16,512]{3,1,2,0:T(2,128)S(1)} collective-permute-done((f32[8,2,16,512]{3,1,2,0:T(2,128)S(1)}, f32[8,2,16,512]{3,1,2,0:T(2,128)S(1)}, u32[]{:S(2)}, u32[]{:S(2)}) %collective-permute-start.5) | collective-permute-done | bytes 524320 | tf_op jit(solution)/shard_map/ppermute | solution.py:13
  182.4 12.8 %collective-permute-done.6 = f32[8,2,16,512]{3,1,2,0:T(2,128)S(1)} collective-permute-done((f32[8,2,16,512]{3,1,2,0:T(2,128)S(1)}, f32[8,2,16,512]{3,1,2,0:T(2,128)S(1)}, u32[]{:S(2)}, u32[]{:S(2)}) %collective-permute-start.6) | collective-permute-done | bytes 524320 | tf_op jit(solution)/shard_map/ppermute | solution.py:13
  195.2 4.5 fusion.38
  201.1 3.3 collective-permute-start.9
  204.3 1.9 collective-permute-start.8
  206.3 12.3 %collective-permute-start.7 = (f32[8,2,16,128]{3,1,2,0:T(2,128)S(1)}, f32[8,2,16,128]{3,1,2,0:T(2,128)S(1)}, u32[]{:S(2)}, u32[]{:S(2)}) collective-permute-start(f32[8,2,16,128]{3,1,2,0:T(2,128)S(1)} %bitcast.386), channel_id=1, source_target_pairs={{0,8},{8,16},{16,24},{24,0},{32,40},{40,48},{48,56},{56,32},{64,72... | collective-permute-start | bytes 393224 | tf_op jit(solution)/shard_map/ppermute | solution.py:13
  224.3 27.1 %psum.14 = f32[]{:T(128)} all-reduce(f32[]{:T(128)S(6)} %add.591), channel_id=1, replica_groups=mesh['chan'=64,'freq'=8] {'freq'}, use_global_device_ids=true, to_apply=%region_9.10 | all-reduce | flops 1 | bytes 8 | tf_op jit(solution)/shard_map/psum | solution.py:124
  251.6 279.1 %psum.15 = f32[]{:T(128)} all-reduce(f32[]{:T(128)} %psum.14), channel_id=1, replica_groups=mesh['chan'=64,'freq'=8] {'chan'}, use_global_device_ids=true, to_apply=%region_10.11 | all-reduce | flops 1 | bytes 8 | tf_op jit(solution)/shard_map/psum | solution.py:124
  531.6 1.2 gather_fusion.1
  532.9 0.9 bitcast_select_fusion
  (228 shorter events, 47.9 us)
Async XLA Ops:
  0.6 26.7 %copy-start.45 = (s32[8192]{0:T(1024)S(1)}, s32[8192]{0:T(1024)}, u32[]{:S(2)}) copy-start(s32[8192]{0:T(1024)} %param.6) | copy-start | bytes 98308
  0.6 27.4 %copy-start.46 = (s32[64]{0:T(128)S(1)}, s32[64]{0:T(128)}, u32[]{:S(2)}) copy-start(s32[64]{0:T(128)} %param.7) | copy-start | bytes 772
  2.6 26.9 %collective-permute-start.1 = (bf16[8,2,24,128]{3,2,1,0:T(8,128)(2,1)}, bf16[8,2,24,128]{3,2,1,0:T(8,128)(2,1)S(1)}, u32[]{:S(2)}, u32[]{:S(2)}) collective-permute-start(bf16[8,2,24,128]{3,2,1,0:T(8,128)(2,1)} %get-tuple-element.57), channel_id=1, source_target_pairs={{0,16},{8,24},{16,0},{24,8},{32,48},{40,56},{48,32},{56,40},{64,80... | collective-permute-start | bytes 294920 | tf_op jit(solution)/shard_map/ppermute | solution.py:13
  18.9 10.7 %collective-permute-start = (bf16[8,2,24,128]{3,2,1,0:T(8,128)(2,1)S(1)}, bf16[8,2,24,128]{3,2,1,0:T(8,128)(2,1)S(1)}, u32[]{:S(2)}, u32[]{:S(2)}) collective-permute-start(bf16[8,2,24,128]{3,2,1,0:T(8,128)(2,1)S(1)} %get-tuple-element.58), channel_id=1, source_target_pairs={{0,8},{8,16},{16,24},{24,0},{32,40},{40,48},{48,56},{56,32},{64,72... | collective-permute-start | bytes 294920 | tf_op jit(solution)/shard_map/ppermute | solution.py:13
  23.6 15.7 %collective-permute-start.2 = (bf16[8,2,24,128]{3,2,1,0:T(8,128)(2,1)S(1)}, bf16[8,2,24,128]{3,2,1,0:T(8,128)(2,1)}, u32[]{:S(2)}, u32[]{:S(2)}) collective-permute-start(bf16[8,2,24,128]{3,2,1,0:T(8,128)(2,1)S(1)} %get-tuple-element.59), channel_id=1, source_target_pairs={{0,24},{8,0},{16,8},{24,16},{32,56},{40,32},{48,40},{56,48},{64,88... | collective-permute-start | bytes 294920 | tf_op jit(solution)/shard_map/ppermute | solution.py:13
  47.4 25.4 %collective-permute-start.4 = (bf16[8,2,24,512]{3,2,1,0:T(8,128)(2,1)}, bf16[8,2,24,512]{3,2,1,0:T(8,128)(2,1)S(1)}, u32[]{:S(2)}, u32[]{:S(2)}) collective-permute-start(bf16[8,2,24,512]{3,2,1,0:T(8,128)(2,1)} %reshape.1311), channel_id=1, source_target_pairs={{0,448},{8,456},{16,464},{24,472},{32,480},{40,488},{48,496},{56,5... | collective-permute-start | bytes 1179656 | tf_op jit(solution)/shard_map/ppermute | solution.py:13
  55.0 17.7 %collective-permute-start.3 = (bf16[8,2,24,512]{3,2,1,0:T(8,128)(2,1)}, bf16[8,2,24,512]{3,2,1,0:T(8,128)(2,1)S(1)}, u32[]{:S(2)}, u32[]{:S(2)}) collective-permute-start(bf16[8,2,24,512]{3,2,1,0:T(8,128)(2,1)} %reshape.1311), channel_id=1, source_target_pairs={{0,480},{8,488},{16,496},{24,504},{32,0},{40,8},{48,16},{56,24},{6... | collective-permute-start | bytes 1179656 | tf_op jit(solution)/shard_map/ppermute | solution.py:13
  72.7 1.9 copy-start.3
  72.8 0.8 copy-start
  74.7 0.9 copy-start.5
  87.0 0.8 copy-start.2
  88.6 9.3 %copy-start.1 = (bf16[8,2,24,512]{3,2,1,0:T(8,128)(2,1)S(1)}, bf16[8,2,24,512]{3,2,1,0:T(8,128)(2,1)}, u32[]{:S(2)}) copy-start(bf16[8,2,24,512]{3,2,1,0:T(8,128)(2,1)} %copy-done) | copy-start | bytes 1179652
  102.4 3.7 slice-start.1
  102.4 3.8 slice-start
  103.5 2.7 slice-start.4
  105.4 1.7 slice-start.2
  106.1 1.7 slice-start.3
  106.2 2.4 copy-start.11
  111.9 3.3 copy-start.10
  118.7 3.3 copy-start.4
  125.8 1.0 copy-start.26
  127.4 1.9 copy-start.9
  131.2 0.9 copy-start.23
  132.7 2.6 copy-start.8
  137.3 0.9 copy-start.21
  138.9 3.4 copy-start.7
  144.2 0.9 copy-start.20
  145.7 3.4 copy-start.6
  151.0 0.9 copy-start.16
  156.7 1.3 copy-start.28
  157.5 1.0 copy-start.12
  157.5 1.1 copy-start.13
  157.6 1.1 copy-start.15
  157.6 1.2 copy-start.17
  157.6 1.3 copy-start.18
  157.6 1.3 copy-start.19
  157.6 1.4 copy-start.22
  157.6 1.5 copy-start.24
  157.6 1.5 copy-start.25
  157.6 1.6 copy-start.27
  163.4 7.2 %copy-start.14 = (bf16[8,2,16,4,128]{4,2,1,3,0:T(8,128)(2,1)S(1)}, bf16[8,2,16,4,128]{4,2,1,3,0:T(8,128)(2,1)}, u32[]{:S(2)}) copy-start(bf16[8,2,16,4,128]{4,2,1,3,0:T(8,128)(2,1)} %copy.71) | copy-start | bytes 786436
  164.0 18.4 %collective-permute-start.5 = (f32[8,2,16,512]{3,1,2,0:T(2,128)S(1)}, f32[8,2,16,512]{3,1,2,0:T(2,128)S(1)}, u32[]{:S(2)}, u32[]{:S(2)}) collective-permute-start(f32[8,2,16,512]{3,1,2,0:T(2,128)S(1)} %get-tuple-element.4), channel_id=1, source_target_pairs={{0,32},{8,40},{16,48},{24,56},{32,64},{40,72},{48,80},{56,88},{64,... | collective-permute-start | bytes 1572872 | tf_op jit(solution)/shard_map/ppermute | solution.py:13
  165.9 29.2 %collective-permute-start.6 = (f32[8,2,16,512]{3,1,2,0:T(2,128)S(1)}, f32[8,2,16,512]{3,1,2,0:T(2,128)S(1)}, u32[]{:S(2)}, u32[]{:S(2)}) collective-permute-start(f32[8,2,16,512]{3,1,2,0:T(2,128)S(1)} %get-tuple-element.5), channel_id=1, source_target_pairs={{0,64},{8,72},{16,80},{24,88},{32,96},{40,104},{48,112},{56,120},{... | collective-permute-start | bytes 1572872 | tf_op jit(solution)/shard_map/ppermute | solution.py:13
  170.6 24.5 %copy-start.39 = (f32[1,8,16,4,128]{4,3,0,2,1:T(4,128)S(1)}, f32[1,8,16,4,128]{4,3,0,2,1:T(4,128)}, u32[]{:S(2)}) copy-start(f32[1,8,16,4,128]{4,3,0,2,1:T(4,128)} %copy.64) | copy-start | bytes 786436
  170.6 24.5 %copy-start.40 = (f32[1,8,16,4,128]{4,3,0,2,1:T(4,128)S(1)}, f32[1,8,16,4,128]{4,3,0,2,1:T(4,128)}, u32[]{:S(2)}) copy-start(f32[1,8,16,4,128]{4,3,0,2,1:T(4,128)} %copy.65) | copy-start | bytes 786436
  170.6 24.5 %copy-start.41 = (f32[1,8,16,4,128]{4,3,0,2,1:T(4,128)S(1)}, f32[1,8,16,4,128]{4,3,0,2,1:T(4,128)}, u32[]{:S(2)}) copy-start(f32[1,8,16,4,128]{4,3,0,2,1:T(4,128)} %copy.69) | copy-start | bytes 786436
  170.7 24.5 %copy-start.42 = (f32[1,8,16,4,128]{4,3,0,2,1:T(4,128)S(1)}, f32[1,8,16,4,128]{4,3,0,2,1:T(4,128)}, u32[]{:S(2)}) copy-start(f32[1,8,16,4,128]{4,3,0,2,1:T(4,128)} %copy.70) | copy-start | bytes 786436
  170.7 24.5 %copy-start.43 = (f32[1,8,16,4,128]{4,3,0,2,1:T(4,128)S(1)}, f32[1,8,16,4,128]{4,3,0,2,1:T(4,128)}, u32[]{:S(2)}) copy-start(f32[1,8,16,4,128]{4,3,0,2,1:T(4,128)} %copy.39) | copy-start | bytes 786436
  170.7 24.5 %copy-start.44 = (f32[1,8,16,4,128]{4,3,0,2,1:T(4,128)S(1)}, f32[1,8,16,4,128]{4,3,0,2,1:T(4,128)}, u32[]{:S(2)}) copy-start(f32[1,8,16,4,128]{4,3,0,2,1:T(4,128)} %copy.40) | copy-start | bytes 786436
  171.2 24.0 %copy-start.29 = (f32[1,8,16,4,128]{4,3,0,2,1:T(4,128)S(1)}, f32[1,8,16,4,128]{4,3,0,2,1:T(4,128)}, u32[]{:S(2)}) copy-start(f32[1,8,16,4,128]{4,3,0,2,1:T(4,128)} %copy.33) | copy-start | bytes 786436
  171.2 24.0 %copy-start.30 = (f32[1,8,16,4,128]{4,3,0,2,1:T(4,128)S(1)}, f32[1,8,16,4,128]{4,3,0,2,1:T(4,128)}, u32[]{:S(2)}) copy-start(f32[1,8,16,4,128]{4,3,0,2,1:T(4,128)} %copy.34) | copy-start | bytes 786436
  171.2 24.0 %copy-start.31 = (f32[1,8,16,4,128]{4,3,0,2,1:T(4,128)S(1)}, f32[1,8,16,4,128]{4,3,0,2,1:T(4,128)}, u32[]{:S(2)}) copy-start(f32[1,8,16,4,128]{4,3,0,2,1:T(4,128)} %copy.44) | copy-start | bytes 786436
  171.2 24.0 %copy-start.32 = (f32[1,8,16,4,128]{4,3,0,2,1:T(4,128)S(1)}, f32[1,8,16,4,128]{4,3,0,2,1:T(4,128)}, u32[]{:S(2)}) copy-start(f32[1,8,16,4,128]{4,3,0,2,1:T(4,128)} %copy.45) | copy-start | bytes 786436
  171.2 24.0 %copy-start.33 = (f32[1,8,16,4,128]{4,3,0,2,1:T(4,128)S(1)}, f32[1,8,16,4,128]{4,3,0,2,1:T(4,128)}, u32[]{:S(2)}) copy-start(f32[1,8,16,4,128]{4,3,0,2,1:T(4,128)} %copy.49) | copy-start | bytes 786436
  171.2 24.0 %copy-start.34 = (f32[1,8,16,4,128]{4,3,0,2,1:T(4,128)S(1)}, f32[1,8,16,4,128]{4,3,0,2,1:T(4,128)}, u32[]{:S(2)}) copy-start(f32[1,8,16,4,128]{4,3,0,2,1:T(4,128)} %copy.50) | copy-start | bytes 786436
  171.2 24.0 %copy-start.35 = (f32[1,8,16,4,128]{4,3,0,2,1:T(4,128)S(1)}, f32[1,8,16,4,128]{4,3,0,2,1:T(4,128)}, u32[]{:S(2)}) copy-start(f32[1,8,16,4,128]{4,3,0,2,1:T(4,128)} %copy.54) | copy-start | bytes 786436
  171.2 24.0 %copy-start.36 = (f32[1,8,16,4,128]{4,3,0,2,1:T(4,128)S(1)}, f32[1,8,16,4,128]{4,3,0,2,1:T(4,128)}, u32[]{:S(2)}) copy-start(f32[1,8,16,4,128]{4,3,0,2,1:T(4,128)} %copy.55) | copy-start | bytes 786436
  171.3 24.0 %copy-start.37 = (f32[1,8,16,4,128]{4,3,0,2,1:T(4,128)S(1)}, f32[1,8,16,4,128]{4,3,0,2,1:T(4,128)}, u32[]{:S(2)}) copy-start(f32[1,8,16,4,128]{4,3,0,2,1:T(4,128)} %copy.59) | copy-start | bytes 786436
  171.3 24.0 %copy-start.38 = (f32[1,8,16,4,128]{4,3,0,2,1:T(4,128)S(1)}, f32[1,8,16,4,128]{4,3,0,2,1:T(4,128)}, u32[]{:S(2)}) copy-start(f32[1,8,16,4,128]{4,3,0,2,1:T(4,128)} %copy.60) | copy-start | bytes 786436
  201.1 330.2 %collective-permute-start.9 = (f32[8,2,16,128]{3,1,2,0:T(2,128)S(1)}, f32[8,2,16,128]{3,1,2,0:T(2,128)S(1)}, u32[]{:S(2)}, u32[]{:S(2)}) collective-permute-start(f32[8,2,16,128]{3,1,2,0:T(2,128)S(1)} %bitcast.390), channel_id=1, source_target_pairs={{0,24},{8,0},{16,8},{24,16},{32,56},{40,32},{48,40},{56,48},{64,88... | collective-permute-start | bytes 393224 | tf_op jit(solution)/shard_map/ppermute | solution.py:13
  204.3 327.0 %collective-permute-start.8 = (f32[8,2,16,128]{3,1,2,0:T(2,128)S(1)}, f32[8,2,16,128]{3,1,2,0:T(2,128)S(1)}, u32[]{:S(2)}, u32[]{:S(2)}) collective-permute-start(f32[8,2,16,128]{3,1,2,0:T(2,128)S(1)} %bitcast.388), channel_id=1, source_target_pairs={{0,16},{8,24},{16,0},{24,8},{32,48},{40,56},{48,32},{56,40},{64,80... | collective-permute-start | bytes 393224 | tf_op jit(solution)/shard_map/ppermute | solution.py:13
  206.3 325.1 %collective-permute-start.7 = (f32[8,2,16,128]{3,1,2,0:T(2,128)S(1)}, f32[8,2,16,128]{3,1,2,0:T(2,128)S(1)}, u32[]{:S(2)}, u32[]{:S(2)}) collective-permute-start(f32[8,2,16,128]{3,1,2,0:T(2,128)S(1)} %bitcast.386), channel_id=1, source_target_pairs={{0,8},{8,16},{16,24},{24,0},{32,40},{40,48},{48,56},{56,32},{64,72... | collective-permute-start | bytes 393224 | tf_op jit(solution)/shard_map/ppermute | solution.py:13
